TPU v7x, 512 devices: a whole 4x4x16 slice. The times are simulated.
512 devices in a mesh: blk: 32 (over z, core), ctr: 16 (over x, y).
Axes of the slice: x: 4, y: 4, z: 16, core: 2. Of those that a mesh axis runs over, the one named last changes fastest.
Arguments:
- integrals: float32 [32, 800, 12800], P('blk', None, 'ctr'), may hold values from -0.078125 to 0.078125
- amplitudes: float32 [8, 12800, 128], P(None, 'ctr', 'blk'), may hold values from -6 to 6
- blockmap: int32 [32], replicated, may hold values from 0 to 31, each once
- vir_energy: float32 [320], replicated, may hold values from 0.2 to 3
- occ_energy: float32 [32], replicated, may hold values from -2 to -0.3
Outputs:
- ladder: float32 [32, 800, 128], P('blk', 'ctr')
- increment: float32 [32, 800, 128], P('blk', 'ctr')
Inputs may be any that keep to these rules, and one draw needn't show every extreme that they name: `blockmap`: every block number appears in exactly one slot.
All inputs are finite; a program needn't handle non-finite values.
Results may differ from a plain program's by a relative error of at most 0.0003.
Values sent between devices are 32-bit elements; how exact they have to be, the bound alone decides.
A program may use at most 64 MiB of HBM per device.

v0:
```python
import jax
import jax.numpy as jnp
from jax import lax
from jax.sharding import PartitionSpec as P

NIRR = 8
VI = 40
OI = 4


def denominator(block, groups, ab_block, start, count, columns, vir_energy, occ_energy):
    irrep = block // groups
    rows = block % groups * ab_block + start + jnp.arange(count, dtype=jnp.int32)
    arow = rows // (VI * VI)
    first = arow * VI + rows // VI % VI
    second = jnp.bitwise_xor(arow, irrep) * VI + rows % VI
    cols = jnp.arange(columns, dtype=jnp.int32)
    orow = cols // (OI * OI)
    hole_one = orow * OI + cols // OI % OI
    hole_two = jnp.bitwise_xor(orow, irrep) * OI + cols % OI
    upper = jnp.take(vir_energy, first) + jnp.take(vir_energy, second)
    lower = jnp.take(occ_energy, hole_one) + jnp.take(occ_energy, hole_two)
    return upper[:, None] - lower[None, :]


def on_device(integrals, amplitudes, blockmap, vir_energy, occ_energy):
    blocks = lax.axis_size("blk")
    groups = blocks // NIRR
    block = blockmap[lax.axis_index("blk")]
    irrep = block // groups
    local = integrals[0]
    ab_block = local.shape[0]
    share = ab_block // lax.axis_size("ctr")
    chosen = lax.dynamic_index_in_dim(
        lax.all_gather(amplitudes, "blk", axis=2, tiled=True), irrep, 0, keepdims=False
    )
    partial_value = jnp.dot(
        local, chosen, preferred_element_type=jnp.float32, precision=lax.Precision.HIGHEST
    )
    offset = lax.axis_index("ctr") * share
    summed = lax.psum(partial_value, "ctr")
    mine = lax.dynamic_slice_in_dim(summed, offset, share, 0)
    denom = denominator(
        block, groups, ab_block, offset, share, partial_value.shape[1], vir_energy, occ_energy
    )
    return (mine[None], (mine / denom)[None])


def solution(mesh):
    placed = (P("blk", None, "ctr"), P(None, "ctr", "blk"), P(), P(), P())
    return jax.shard_map(
        on_device,
        mesh=mesh,
        in_specs=placed,
        out_specs=(P("blk", "ctr", None), P("blk", "ctr", None)),
        check_vma=False,
    )
```

profile of v0, /device:TPU:1, one launch (start us, length us, event | category | flops | bytes accessed | tf_op | source)
XLA Modules:
  0.0 216.9 jit_solution(8008306709315105640)
XLA Ops:
  7.2 0.0 copy-start
  7.2 0.0 all-gather.2.cloned.1.call-start
  7.2 1.7 copy.11
  8.9 0.0 all-gather.2.cloned.1.call-update
  9.0 0.0 all-reduce.2.cloned.1.call-start
  9.0 1.2 dynamic_slice.10
  12.9 1.5 gather_fusion
  14.4 1.5 gather_fusion.1
  15.9 1.6 gather_fusion.3
  17.5 1.6 gather_fusion.2
  19.1 70.3 %all-gather.2.cloned.1.call-done = f32[8,800,128]{1,0,2:T(8,128)} async-done(((f32[8,800,4]{1,0,2:T(8,128)}), f32[8,800,128]{1,0,2:T(8,128)}) %all-gather.2.cloned.1.call-update) | async-done | bytes 3276816 | tf_op jit(solution)/shard_map/all_gather | solution.py:35
  89.4 2.4 %constant_dynamic-slice_fusion.1 = f32[1,800,128]{1,0,2:T(1,128)S(1)} fusion(f32[8,800,128]{1,0,2:T(8,128)} %all-gather.2.cloned.1.call-done, s32[]{:T(128)S(6)} %select_n.74), kind=kLoop, calls=%fused_computation.47 | loop fusion | bytes 819204 | tf_op jit(solution)/shard_map/jit(dynamic_index_in_dim)/dynamic_slice | solution.py:34
  91.8 1.1 copy.14
  92.9 0.0 copy-done
  92.9 4.2 %fusion.2 = f32[800,128]{1,0:T(8,128)} fusion(f32[1,800,800]{2,1,0:T(8,128)S(1)} %copy-done, f32[1,800,128]{2,1,0:T(8,128)} %copy.14), kind=kOutput, calls=%fused_computation.6 | convolution fusion | flops 983040000 | bytes 3379200 | tf_op jit(solution)/shard_map/dot_general | solution.py:37
  97.1 0.0 all-reduce.2.cloned.1.call-update
  97.2 110.7 %all-reduce.2.cloned.1.call-done = f32[800,128]{1,0:T(8,128)} async-done(((f32[800,128]{1,0:T(8,128)}), f32[800,128]{1,0:T(8,128)}) %all-reduce.2.cloned.1.call-update) | async-done | bytes 409616 | tf_op jit(solution)/shard_map/psum | solution.py:41
  207.9 0.8 divide_bitcast_fusion
  208.8 0.6 copy.13
  209.4 0.6 broadcast_in_dim.20
  (9 shorter events, 0.1 us)
Async XLA Ops:
  7.2 85.8 %copy-start = (f32[1,800,800]{2,1,0:T(8,128)S(1)}, f32[1,800,800]{2,1,0:T(8,128)}, u32[]{:S(2)}) copy-start(f32[1,800,800]{2,1,0:T(8,128)} %param.9) | copy-start | bytes 7680004
  7.2 82.3 %all-gather.2.cloned.1.call-start = ((), (), s32[]{:S(2)}) async-start(), calls=%async_computation | async-start | bytes 3784704 | tf_op jit(solution)/shard_map/all_gather | solution.py:35
  9.0 199.0 %all-reduce.2.cloned.1.call-start = ((), (), s32[]{:S(2)}) async-start(), calls=%async_computation.1 | async-start | bytes 819200 | tf_op jit(solution)/shard_map/psum | solution.py:41
Sparse Core Ops, SparseCore 0:
  10.1 79.2 all-gather.1
  97.3 110.6 all-reduce.1
where the time goes:
time: 217 us
  waiting for transfers between devices  181 us (83%)
  between operations  16.7 us (8%)
  local copies, waits for them, and re-layouts  13.8 us (6%)
  matrix products  4.2 us (2%)
    psum x1, waiting for transfers between devices, on_device(): summed = lax.psum(partial_value, 'ctr')  111 us
    all_gather x1, waiting for transfers between devices, on_device(): lax.all_gather(amplitudes, 'blk', axis=2, tiled=True)  70.3 us
  transfers between devices with their start and end apart: 2, of which 2 were waited for; matrix products, arithmetic and copies ran while one was open for 3% of the time, Pallas kernels for 0%

commit v1 on v0

v1 whole, which is shorter than its diff:
```python
import functools

import jax
import jax.numpy as jnp
from jax import lax
from jax.experimental import pallas as pl
from jax.experimental.pallas import tpu as pltpu
from jax.sharding import PartitionSpec as P

NIRR = 8
VI = 40
OI = 4
MESH = pl.DeviceIdType.MESH
NT = (((1,), (1,)), ((), ()))


def denominator(block, groups, ab_block, start, count, columns, vir, occ_ref):
    irrep = block // groups
    quarter = block - irrep * groups
    rows = quarter * ab_block + start + lax.broadcasted_iota(jnp.int32, (count, 1), 0)
    first = (rows * 52429) >> 21
    digit = rows - first * VI
    arow = (first * 52429) >> 21
    second = jnp.bitwise_xor(arow, irrep) * VI + digit
    index = lax.broadcasted_iota(jnp.int32, (1, vir.shape[1]), 1)
    up_one = jnp.sum(jnp.where(index == first, vir, 0.0), axis=1, keepdims=True)
    up_two = jnp.sum(jnp.where(index == second, vir, 0.0), axis=1, keepdims=True)
    cols = lax.broadcasted_iota(jnp.int32, (1, columns), 1)
    hole_one = cols >> 2
    hole_two = jnp.bitwise_xor(cols >> 4, irrep) * OI + (cols & 3)
    low_one = jnp.zeros((1, columns), jnp.float32)
    low_two = jnp.zeros((1, columns), jnp.float32)
    for o in range(NIRR * OI):
        low_one = jnp.where(hole_one == o, occ_ref[o], low_one)
        low_two = jnp.where(hole_two == o, occ_ref[o], low_two)
    return (up_one + up_two) - (low_one + low_two)


def kernel(
    nb, nc, blockmap_ref, occ_ref, vir_ref, amps_ref, ints_hbm,
    ladder_ref, incr_ref,
    ints_f32, ints_hi, ints_lo, outbox, inbox, gathered, partial_sum, sums_out, sums_in, denom_ref,
    ints_sem, a_send, a_recv, s_send, s_recv,
):
    b = lax.axis_index("blk")
    c = lax.axis_index("ctr")
    groups = nb // NIRR
    ab, cd = ints_f32.shape
    share = ab // nc
    mine = amps_ref.shape[1]
    ints_copy = pltpu.make_async_copy(ints_hbm, ints_f32, ints_sem)
    ints_copy.start()

    barrier = pltpu.get_barrier_semaphore()

    @pl.loop(1, nb)
    def _(k):
        pl.semaphore_signal(barrier, inc=1, device_id=(lax.rem(b + k, nb), c), device_id_type=MESH)

    @pl.loop(1, nc)
    def _(k):
        pl.semaphore_signal(barrier, inc=1, device_id=(b, lax.rem(c + k, nc)), device_id_type=MESH)

    for p in range(nb):
        outbox[p] = amps_ref[blockmap_ref[p] // groups]
    pl.semaphore_wait(barrier, nb - 1 + nc - 1)

    def amps_copy(k):
        to = lax.rem(b + k, nb)
        return pltpu.make_async_remote_copy(
            src_ref=outbox.at[to], dst_ref=inbox.at[b], send_sem=a_send.at[k], recv_sem=a_recv.at[k],
            device_id=(to, c), device_id_type=MESH,
        )

    @pl.loop(0, nb - 1)
    def _(i):
        k = nb // 2 + ((i + 1) // 2) * (2 * (i % 2) - 1)
        amps_copy(k).start()

    inbox[b] = amps_ref[blockmap_ref[b] // groups]
    denom_ref[...] = denominator(
        blockmap_ref[b], groups, ab, c * share, share, nb * mine, vir_ref[...], occ_ref
    )
    ints_copy.wait()
    value = ints_f32[...]
    high = value.astype(jnp.bfloat16)
    ints_hi[...] = high
    ints_lo[...] = (value - high.astype(jnp.float32)).astype(jnp.bfloat16)

    @pl.loop(1, nb)
    def _(k):
        amps_copy(k).wait_recv()

    for p in range(nb):
        gathered[p * mine:(p + 1) * mine, :] = inbox[p]
    amps = gathered[...]
    amps_hi = amps.astype(jnp.bfloat16)
    amps_lo = (amps - amps_hi.astype(jnp.float32)).astype(jnp.bfloat16)
    dot = functools.partial(lax.dot_general, dimension_numbers=NT, preferred_element_type=jnp.float32)
    step = 160
    for r in range(0, ab, step):
        high = ints_hi[r:r + step, :]
        partial_sum[r:r + step, :] = (
            dot(ints_lo[r:r + step, :], amps_hi) + dot(high, amps_lo) + dot(high, amps_hi)
        )
    for p in range(nc):
        sums_out[p] = partial_sum[p * share:(p + 1) * share, :]

    def sums_copy(k):
        to = lax.rem(c + k, nc)
        return pltpu.make_async_remote_copy(
            src_ref=sums_out.at[to], dst_ref=sums_in.at[c], send_sem=s_send.at[k], recv_sem=s_recv.at[k],
            device_id=(b, to), device_id_type=MESH,
        )

    @pl.loop(1, nc)
    def _(k):
        sums_copy(k).start()

    sums_in[c] = sums_out[c]

    @pl.loop(1, nc)
    def _(k):
        sums_copy(k).wait_recv()

    total = sums_in[0]
    for p in range(1, nc):
        total = total + sums_in[p]
    ladder_ref[...] = total
    incr_ref[...] = total / denom_ref[...]

    @pl.loop(1, nb)
    def _(k):
        amps_copy(k).wait_send()

    @pl.loop(1, nc)
    def _(k):
        sums_copy(k).wait_send()


def on_device(integrals, amplitudes, blockmap, vir_energy, occ_energy):
    nb, nc = lax.axis_size("blk"), lax.axis_size("ctr")
    _, ab, cd = integrals.shape
    irreps, _, mine = amplitudes.shape
    ij = mine * nb
    share = ab // nc
    vmem = pl.BlockSpec(memory_space=pltpu.VMEM)
    smem = pl.BlockSpec(memory_space=pltpu.SMEM)
    out = jax.ShapeDtypeStruct((share, ij), jnp.float32)
    ladder, increment = pl.pallas_call(
        functools.partial(kernel, nb, nc),
        out_shape=(out, out),
        in_specs=[smem, smem, vmem, vmem, pl.BlockSpec(memory_space=pl.ANY)],
        out_specs=(vmem, vmem),
        scratch_shapes=[
            pltpu.VMEM((ab, cd), jnp.float32),
            pltpu.VMEM((ab, cd), jnp.bfloat16),
            pltpu.VMEM((ab, cd), jnp.bfloat16),
            pltpu.VMEM((nb, mine, cd), jnp.float32),
            pltpu.VMEM((nb, mine, cd), jnp.float32),
            pltpu.VMEM((ij, cd), jnp.float32),
            pltpu.VMEM((ab, ij), jnp.float32),
            pltpu.VMEM((nc, share, ij), jnp.float32),
            pltpu.VMEM((nc, share, ij), jnp.float32),
            pltpu.VMEM((share, ij), jnp.float32),
            pltpu.SemaphoreType.DMA,
            pltpu.SemaphoreType.DMA((nb,)),
            pltpu.SemaphoreType.DMA((nb,)),
            pltpu.SemaphoreType.DMA((nc,)),
            pltpu.SemaphoreType.DMA((nc,)),
        ],
        compiler_params=pltpu.CompilerParams(
            collective_id=0, has_side_effects=True, vmem_limit_bytes=48 << 20
        ),
    )(
        blockmap, occ_energy, vir_energy[None, :], jnp.transpose(amplitudes, (0, 2, 1)), integrals[0]
    )
    return ladder[None], increment[None]


def solution(mesh):
    placed = (P("blk", None, "ctr"), P(None, "ctr", "blk"), P(), P(), P())
    return jax.shard_map(
        on_device,
        mesh=mesh,
        in_specs=placed,
        out_specs=(P("blk", "ctr", None), P("blk", "ctr", None)),
        check_vma=False,
    )
```

time: 217 us -> 56.9 us (0.26)
  waiting for transfers between devices: 181 us -> 0 us
  Pallas kernels: 0 us -> 50.1 us
  between operations: 16.7 us -> 0.64 us
  local copies, waits for them, and re-layouts: 13.8 us -> 5.97 us
  matrix products: 4.2 us -> 0 us
    psum x1 -> x0, waiting for transfers between devices: 111 us -> none  [on_device(): summed = lax.psum(partial_value, 'ctr')]
    all_gather x1 -> x0, waiting for transfers between devices: 70.3 us -> none  [on_device(): lax.all_gather(amplitudes, 'blk', axis=2, tiled=True)]
    pallas_call x0 -> x1, Pallas kernels: none -> 50.1 us  [on_device(): pl.pallas_call(functools.partial(kernel, nb, nc), out_shape=(out, out), i...]
    gather x4 -> x0, local copies, waits for them, and re-layouts: 6.13 us -> none  [the longest x2 3.17 us: denominator(): lower = jnp.take(occ_energy, hole_one) + jnp.take(occ_energy, hole_two)]
    dot_general x1 -> x0, matrix products: 4.2 us -> none  [on_device(): jnp.dot(local, chosen, preferred_element_type=jnp.float32, precision=lax....]
    dynamic_slice x2 -> x0, local copies, waits for them, and re-layouts: 3.6 us -> none  [the longest x1 2.35 us: on_device(): lax.dynamic_index_in_dim(lax.all_gather(amplitudes, 'blk', axis=2, tiled=...]
    unnamed x5 -> x10, local copies, waits for them, and re-layouts: 3.47 us -> 5.29 us
  transfers between devices with their start and end apart: 2 -> 0, of which waited for: 2 -> 0; matrix products, arithmetic and copies ran while one was open for 3% -> 0% of each run, Pallas kernels for 0% -> 0%
where the time goes in v1:
time: 56.9 us; the launch traced here: 56.7 us
  Pallas kernels  50.1 us (88%)
  local copies, waits for them, and re-layouts  5.97 us (10%)
  between operations  0.64 us (1%)
    pallas_call x1, Pallas kernels, on_device(): pl.pallas_call(functools.partial(kernel, nb, nc), out_shape=(out, out), i...  50.1 us
    unnamed x10, local copies, waits for them, and re-layouts  5.29 us

profile of v1, /device:TPU:1, one launch (start us, length us, event | category | flops | bytes accessed | tf_op | source)
XLA Modules:
  0.0 56.7 jit_solution(852007254603553269)
XLA Ops:
  0.6 0.7 %broadcast_in_dim.9.vir_ref = f32[1,320]{1,0:T(1,128)S(1)} reshape(f32[320]{0:T(512)} %param.8) | data formatting | bytes 2560 | tf_op jit(solution)/shard_map/broadcast_in_dim | solution.py:176
  1.3 0.0 copy-start
  1.3 1.8 %copy-done = f32[1,800,800]{2,1,0:T(8,128)S(1)} copy-done((f32[1,800,800]{2,1,0:T(8,128)S(1)}, f32[1,800,800]{2,1,0:T(8,128)}, u32[]{:S(2)}) %copy-start) | copy-done | bytes 2560024
  3.1 0.0 copy-start.1
  3.1 0.9 %copy-done.1 = f32[8,800,4]{1,2,0:T(4,128)S(1)} copy-done((f32[8,800,4]{1,2,0:T(4,128)S(1)}, f32[8,800,4]{1,2,0:T(4,128)}, u32[]{:S(2)}) %copy-start.1) | copy-done | bytes 102424
  4.0 0.0 copy-start.2
  4.0 0.7 %copy-done.2 = s32[32]{0:T(128)S(1)} copy-done((s32[32]{0:T(128)S(1)}, s32[32]{0:T(128)}, u32[]{:S(2)}) %copy-start.2) | copy-done | bytes 152
  4.7 0.0 copy-start.3
  4.7 0.7 %copy-done.3 = f32[32]{0:T(128)S(1)} copy-done((f32[32]{0:T(128)S(1)}, f32[32]{0:T(128)}, u32[]{:S(2)}) %copy-start.3) | copy-done | bytes 152
  5.3 50.1 %shard_map.68 = (f32[50,128]{1,0:T(8,128)S(1)}, f32[50,128]{1,0:T(8,128)S(1)}) custom-call(s32[32]{0:T(128)S(1)} %copy-done.2, f32[32]{0:T(128)S(1)} %copy-done.3, f32[1,320]{1,0:T(1,128)S(1)} %broadcast_in_dim.9.vir_ref, f32[8,4,800]{2,1,0:T(4,128)S(1)} %bitcast.5, f32[800,800]{1,0:T(8,128)S(1)} %bitcast.4), custom_call_target="tpu_custom_call" | custom-call | tf_op jit(solution)/shard_map/pallas_call | solution.py:150
  55.4 0.6 %copy.7 = f32[1,50,128]{2,0,1:T(1,128)} copy(f32[1,50,128]{2,1,0:T(8,128)S(1)} %bitcast.7) | data formatting | bytes 51200
  56.1 0.6 %copy.8 = f32[1,50,128]{2,0,1:T(1,128)} copy(f32[1,50,128]{2,1,0:T(8,128)S(1)} %bitcast.6) | data formatting | bytes 51200
Async XLA Ops:
  1.3 1.8 %copy-start = (f32[1,800,800]{2,1,0:T(8,128)S(1)}, f32[1,800,800]{2,1,0:T(8,128)}, u32[]{:S(2)}) copy-start(f32[1,800,800]{2,1,0:T(8,128)} %param.5) | copy-start | bytes 7680004
  3.1 0.9 %copy-start.1 = (f32[8,800,4]{1,2,0:T(4,128)S(1)}, f32[8,800,4]{1,2,0:T(4,128)}, u32[]{:S(2)}) copy-start(f32[8,800,4]{1,2,0:T(4,128)} %param.6) | copy-start | bytes 307204
  4.0 0.7 %copy-start.2 = (s32[32]{0:T(128)S(1)}, s32[32]{0:T(128)}, u32[]{:S(2)}) copy-start(s32[32]{0:T(128)} %blockmap_ref.1) | copy-start | bytes 388
  4.7 0.7 %copy-start.3 = (f32[32]{0:T(128)S(1)}, f32[32]{0:T(128)}, u32[]{:S(2)}) copy-start(f32[32]{0:T(128)} %occ_ref.1) | copy-start | bytes 388

commit v2 on v1

--- a/solution.py
+++ b/solution.py
@@ -36,60 +36,110 @@
     return (up_one + up_two) - (low_one + low_two)
 
 
+def rank_of(b):
+    z, core = b // 2, b % 2
+    place = jnp.where(z < 7, z, jnp.where(z < 11, 2 * z - 6, 37 - 2 * z))
+    return 2 * place + core
+
+
+def at_rank(rank):
+    place, core = rank // 2, rank % 2
+    z = jnp.where(place < 7, place, jnp.where(place % 2 == 1, 15 - (place - 7) // 2, 7 + (place - 8) // 2))
+    return 2 * z + core
+
+
 def kernel(
-    nb, nc, blockmap_ref, occ_ref, vir_ref, amps_ref, ints_hbm,
+    nb, nc, blockmap_hbm, occ_hbm, vir_hbm, amps_hbm, ints_hbm,
     ladder_ref, incr_ref,
+    blockmap_ref, occ_ref, vir_ref, amps_ref,
     ints_f32, ints_hi, ints_lo, outbox, inbox, gathered, partial_sum, sums_out, sums_in, denom_ref,
-    ints_sem, a_send, a_recv, s_send, s_recv,
+    fetch_sem, a_send, a_recv, s_send, s_recv, a_ready, s_ready,
 ):
     b = lax.axis_index("blk")
     c = lax.axis_index("ctr")
+    rank = rank_of(b)
     groups = nb // NIRR
     ab, cd = ints_f32.shape
     share = ab // nc
     mine = amps_ref.shape[1]
-    ints_copy = pltpu.make_async_copy(ints_hbm, ints_f32, ints_sem)
-    ints_copy.start()
+    fetches = [
+        pltpu.make_async_copy(src, dst, fetch_sem.at[i])
+        for i, (src, dst) in enumerate(
+            [(blockmap_hbm, blockmap_ref), (amps_hbm, amps_ref), (occ_hbm, occ_ref), (vir_hbm, vir_ref.at[0]),
+             (ints_hbm, ints_f32)]
+        )
+    ]
+    for fetch in fetches:
+        fetch.start()
 
     barrier = pltpu.get_barrier_semaphore()
 
-    @pl.loop(1, nb)
-    def _(k):
-        pl.semaphore_signal(barrier, inc=1, device_id=(lax.rem(b + k, nb), c), device_id_type=MESH)
-
-    @pl.loop(1, nc)
-    def _(k):
-        pl.semaphore_signal(barrier, inc=1, device_id=(b, lax.rem(c + k, nc)), device_id_type=MESH)
-
-    for p in range(nb):
-        outbox[p] = amps_ref[blockmap_ref[p] // groups]
-    pl.semaphore_wait(barrier, nb - 1 + nc - 1)
-
-    def amps_copy(k):
-        to = lax.rem(b + k, nb)
+    @pl.loop(rank + 1, nb)
+    def _(r):
+        pl.semaphore_signal(barrier, inc=1, device_id=(at_rank(r), c), device_id_type=MESH)
+
+    @pl.loop(c + 1, nc)
+    def _(p):
+        pl.semaphore_signal(barrier, inc=1, device_id=(b, p), device_id_type=MESH)
+
+    @pl.when(rank + c > 0)
+    def _():
+        pl.semaphore_wait(barrier, rank + c)
+
+    @pl.loop(0, rank)
+    def _(r):
+        pl.semaphore_signal(a_ready.at[b], inc=1, device_id=(at_rank(r), c), device_id_type=MESH)
+
+    @pl.loop(0, c)
+    def _(p):
+        pl.semaphore_signal(s_ready, inc=1, device_id=(b, p), device_id_type=MESH)
+
+    def amps_copy(to):
         return pltpu.make_async_remote_copy(
-            src_ref=outbox.at[to], dst_ref=inbox.at[b], send_sem=a_send.at[k], recv_sem=a_recv.at[k],
+            src_ref=outbox.at[to], dst_ref=inbox.at[b], send_sem=a_send.at[to], recv_sem=a_recv.at[b],
             device_id=(to, c), device_id_type=MESH,
         )
 
-    @pl.loop(0, nb - 1)
-    def _(i):
-        k = nb // 2 + ((i + 1) // 2) * (2 * (i % 2) - 1)
-        amps_copy(k).start()
+    def amps_arrival(p):
+        return pltpu.make_async_remote_copy(
+            src_ref=outbox.at[p], dst_ref=inbox.at[p], send_sem=a_send.at[p], recv_sem=a_recv.at[p],
+            device_id=(p, c), device_id_type=MESH,
+        )
+
+    fetches[0].wait()
+    fetches[1].wait()
+
+    def send_amps(to):
+        outbox[to] = amps_ref[blockmap_ref[to] // groups]
+        amps_copy(to).start()
+
+    @pl.loop(0, rank)
+    def _(r):
+        send_amps(at_rank(r))
+
+    @pl.loop(rank + 1, nb)
+    def _(r):
+        to = at_rank(r)
+        pl.semaphore_wait(a_ready.at[to], 1)
+        send_amps(to)
 
     inbox[b] = amps_ref[blockmap_ref[b] // groups]
+    fetches[2].wait()
+    fetches[3].wait()
     denom_ref[...] = denominator(
         blockmap_ref[b], groups, ab, c * share, share, nb * mine, vir_ref[...], occ_ref
     )
-    ints_copy.wait()
+    fetches[4].wait()
     value = ints_f32[...]
     high = value.astype(jnp.bfloat16)
     ints_hi[...] = high
     ints_lo[...] = (value - high.astype(jnp.float32)).astype(jnp.bfloat16)
 
-    @pl.loop(1, nb)
-    def _(k):
-        amps_copy(k).wait_recv()
+    @pl.loop(0, nb)
+    def _(p):
+        @pl.when(p != b)
+        def _():
+            amps_arrival(p).wait_recv()
 
     for p in range(nb):
         gathered[p * mine:(p + 1) * mine, :] = inbox[p]
@@ -113,6 +163,10 @@
             device_id=(b, to), device_id_type=MESH,
         )
 
+    @pl.when(c < nc - 1)
+    def _():
+        pl.semaphore_wait(s_ready, nc - 1 - c)
+
     @pl.loop(1, nc)
     def _(k):
         sums_copy(k).start()
@@ -126,12 +180,14 @@
     total = sums_in[0]
     for p in range(1, nc):
         total = total + sums_in[p]
-    ladder_ref[...] = total
-    incr_ref[...] = total / denom_ref[...]
-
-    @pl.loop(1, nb)
-    def _(k):
-        amps_copy(k).wait_send()
+    ladder_ref[:, 0, :] = total
+    incr_ref[:, 0, :] = total / denom_ref[...]
+
+    @pl.loop(0, nb)
+    def _(p):
+        @pl.when(p != b)
+        def _():
+            amps_copy(p).wait_send()
 
     @pl.loop(1, nc)
     def _(k):
@@ -145,14 +201,18 @@
     ij = mine * nb
     share = ab // nc
     vmem = pl.BlockSpec(memory_space=pltpu.VMEM)
-    smem = pl.BlockSpec(memory_space=pltpu.SMEM)
-    out = jax.ShapeDtypeStruct((share, ij), jnp.float32)
+    hbm = pl.BlockSpec(memory_space=pl.ANY)
+    out = jax.ShapeDtypeStruct((share, 1, ij), jnp.float32)
     ladder, increment = pl.pallas_call(
         functools.partial(kernel, nb, nc),
         out_shape=(out, out),
-        in_specs=[smem, smem, vmem, vmem, pl.BlockSpec(memory_space=pl.ANY)],
+        in_specs=[hbm] * 5,
         out_specs=(vmem, vmem),
         scratch_shapes=[
+            pltpu.SMEM(blockmap.shape, jnp.int32),
+            pltpu.SMEM(occ_energy.shape, jnp.float32),
+            pltpu.VMEM((1, vir_energy.shape[0]), jnp.float32),
+            pltpu.VMEM((irreps, mine, cd), jnp.float32),
             pltpu.VMEM((ab, cd), jnp.float32),
             pltpu.VMEM((ab, cd), jnp.bfloat16),
             pltpu.VMEM((ab, cd), jnp.bfloat16),
@@ -163,19 +223,21 @@
             pltpu.VMEM((nc, share, ij), jnp.float32),
             pltpu.VMEM((nc, share, ij), jnp.float32),
             pltpu.VMEM((share, ij), jnp.float32),
-            pltpu.SemaphoreType.DMA,
+            pltpu.SemaphoreType.DMA((5,)),
             pltpu.SemaphoreType.DMA((nb,)),
             pltpu.SemaphoreType.DMA((nb,)),
             pltpu.SemaphoreType.DMA((nc,)),
             pltpu.SemaphoreType.DMA((nc,)),
+            pltpu.SemaphoreType.REGULAR((nb,)),
+            pltpu.SemaphoreType.REGULAR,
         ],
         compiler_params=pltpu.CompilerParams(
-            collective_id=0, has_side_effects=True, vmem_limit_bytes=48 << 20
+            collective_id=0, has_side_effects=True, vmem_limit_bytes=60 << 20
         ),
     )(
-        blockmap, occ_energy, vir_energy[None, :], jnp.transpose(amplitudes, (0, 2, 1)), integrals[0]
+        blockmap, occ_energy, vir_energy, jnp.transpose(amplitudes, (0, 2, 1)), integrals[0]
     )
-    return ladder[None], increment[None]
+    return jnp.transpose(ladder, (1, 0, 2)), jnp.transpose(increment, (1, 0, 2))
 
 
 def solution(mesh):

time: 56.9 us -> 51.5 us (0.905)
  the two profiles are of different devices: /device:TPU:1 before, /device:TPU:352 now
where the time goes in v2:
time: 51.5 us; the launch traced here: 51.2 us
  Pallas kernels  47.9 us (93%)
  local copies, waits for them, and re-layouts  2.7 us (5%)
  between operations  0.64 us (1%)
    pallas_call x1, Pallas kernels, on_device(): pl.pallas_call(functools.partial(kernel, nb, nc), out_shape=(out, out), i...  47.9 us
    unnamed x2, local copies, waits for them, and re-layouts  2.7 us

profile of v2, /device:TPU:352, one launch (start us, length us, event | category | flops | bytes accessed | tf_op | source)
XLA Modules:
  0.0 51.2 jit_solution(14526857086276844038)
XLA Ops:
  0.6 47.9 %shard_map.68 = (f32[50,1,128]{2,1,0:T(1,128)}, f32[50,1,128]{2,1,0:T(1,128)}) custom-call(s32[32]{0:T(128)} %blockmap_hbm.1, f32[32]{0:T(128)} %occ_hbm.1, f32[320]{0:T(512)} %vir_hbm.1, f32[8,4,800]{2,1,0:T(4,128)} %bitcast.5, f32[800,800]{1,0:T(8,128)} %bitcast.4), custom_call_target="tpu_custom_call" | custom-call | tf_op jit(solution)/shard_map/pallas_call | solution.py:206
  48.5 1.4 %copy.9 = f32[1,50,128]{2,0,1:T(1,128)} copy(f32[1,50,128]{2,0,1:T(1,128)} %bitcast.7) | data formatting | bytes 51200
  49.9 1.3 %copy.10 = f32[1,50,128]{2,0,1:T(1,128)} copy(f32[1,50,128]{2,0,1:T(1,128)} %bitcast.6) | data formatting | bytes 51200

commit v3 on v2

v3 whole, which is shorter than its diff:
```python
import functools

import jax
import jax.numpy as jnp
from jax import lax
from jax.experimental import pallas as pl
from jax.experimental.pallas import tpu as pltpu
from jax.sharding import PartitionSpec as P

NIRR = 8
VI = 40
OI = 4
LANES = 128
MESH = pl.DeviceIdType.MESH
CHUNKS = 2
VLIM = 52 << 20
NT = (((1,), (1,)), ((), ()))


def denominator(block, groups, ab_block, start, count, columns, vir, occ_ref):
    irrep = block >> 2
    quarter = block - irrep * groups
    rows = quarter * ab_block + start + lax.broadcasted_iota(jnp.int32, (count, 1), 0)
    first = (rows * 52429) >> 21
    digit = rows - first * VI
    arow = (first * 52429) >> 21
    second = jnp.bitwise_xor(arow, irrep) * VI + digit
    index = lax.broadcasted_iota(jnp.int32, (1, vir.shape[1]), 1)
    up_one = jnp.sum(jnp.where(index == first, vir, 0.0), axis=1, keepdims=True)
    up_two = jnp.sum(jnp.where(index == second, vir, 0.0), axis=1, keepdims=True)
    cols = lax.broadcasted_iota(jnp.int32, (1, columns), 1)
    hole_one = cols >> 2
    hole_two = jnp.bitwise_xor(cols >> 4, irrep) * OI + (cols & 3)
    low_one = jnp.zeros((1, columns), jnp.float32)
    low_two = jnp.zeros((1, columns), jnp.float32)
    for o in range(NIRR * OI):
        low_one = jnp.where(hole_one == o, occ_ref[o], low_one)
        low_two = jnp.where(hole_two == o, occ_ref[o], low_two)
    return (up_one + up_two) - (low_one + low_two)


def rank_of(b):
    z = b >> 1
    return 2 * jnp.where(z < 7, z, jnp.where(z < 11, 2 * z - 6, 37 - 2 * z)) + (b & 1)


def at_rank(rank):
    place = rank >> 1
    half = (place - 7) >> 1
    z = jnp.where(place < 7, place, jnp.where((place & 1) == 1, 15 - half, 7 + half))
    return 2 * z + (rank & 1)


def kernel(
    nb, nc, blockmap_hbm, occ_hbm, vir_hbm, amps_hbm, ints_hbm,
    ladder_ref, incr_ref,
    blockmap_ref, occ_ref, vir_ref, amps_ref,
    ints_f32, ints_hi, ints_lo, packed, outbox, inbox, gathered, product, sums_out, sums_in,
    totals, denom_ref, fetch_sem, a_send, a_recv, s_send, s_recv, a_ready, s_ready,
):
    b = lax.axis_index("blk")
    c = lax.axis_index("ctr")
    rank = rank_of(b)
    early = 14
    groups = nb // NIRR
    ab, cd = ints_f32.shape
    share = ab // nc
    irreps, mine, _ = amps_ref.shape
    full = cd // LANES
    rest = cd - full * LANES
    ij = nb * mine
    width = ij // CHUNKS
    height = sums_out.shape[2]
    starts = [min(g * height, share - height) for g in range(CHUNKS)]
    fetches = [
        pltpu.make_async_copy(src, dst, fetch_sem.at[i])
        for i, (src, dst) in enumerate(
            [(blockmap_hbm, blockmap_ref), (amps_hbm, amps_ref), (occ_hbm, occ_ref), (vir_hbm, vir_ref.at[0]),
             (ints_hbm, ints_f32)]
        )
    ]
    for fetch in fetches:
        fetch.start()

    barrier = pltpu.get_barrier_semaphore()

    @pl.loop(rank + 1, nb)
    def _(r):
        pl.semaphore_signal(barrier, inc=1, device_id=(at_rank(r), c), device_id_type=MESH)

    @pl.loop(c + 1, nc)
    def _(p):
        pl.semaphore_signal(barrier, inc=1, device_id=(b, p), device_id_type=MESH)

    @pl.when(rank + c > 0)
    def _():
        pl.semaphore_wait(barrier, rank + c)

    @pl.loop(0, rank)
    def _(r):
        pl.semaphore_signal(a_ready.at[b], inc=1, device_id=(at_rank(r), c), device_id_type=MESH)

    @pl.loop(0, c)
    def _(p):
        pl.semaphore_signal(s_ready, inc=1, device_id=(b, p), device_id_type=MESH)

    fetches[0].wait()
    fetches[1].wait()
    for h in range(irreps):
        for t in range(full):
            packed[h, t * mine:(t + 1) * mine, :] = amps_ref[h, :, t * LANES:(t + 1) * LANES]
        packed[h, full * mine:full * mine + 1, :] = jnp.concatenate(
            [amps_ref[h, u:u + 1, full * LANES:cd] for u in range(mine)], axis=1
        )

    def amps_copy(to):
        return pltpu.make_async_remote_copy(
            src_ref=outbox.at[to], dst_ref=inbox.at[b], send_sem=a_send.at[to], recv_sem=a_recv.at[b],
            device_id=(to, c), device_id_type=MESH,
        )

    def amps_arrival(p):
        return pltpu.make_async_remote_copy(
            src_ref=outbox.at[p], dst_ref=inbox.at[p], send_sem=a_send.at[p], recv_sem=a_recv.at[p],
            device_id=(p, c), device_id_type=MESH,
        )

    def visit(to):
        @pl.when(rank_of(to) > rank)
        def _():
            pl.semaphore_wait(a_ready.at[to], 1)

        outbox[to] = packed[blockmap_ref[to] >> 2]
        amps_copy(to).start()

    def far(i):
        return (b + nb // 2 + ((i + 1) >> 1) * (2 * (i & 1) - 1)) & (nb - 1)

    @pl.when(rank < early)
    def _():
        @pl.loop(0, early)
        def _(r):
            @pl.when(r != rank)
            def _():
                visit(at_rank(r))

    @pl.when(rank >= early)
    def _():
        @pl.loop(0, nb - 1)
        def _(i):
            to = far(i)

            @pl.when(rank_of(to) < early)
            def _():
                visit(to)

    @pl.loop(0, nb - 1)
    def _(i):
        to = far(i)

        @pl.when(rank_of(to) >= early)
        def _():
            visit(to)

    inbox[b] = packed[blockmap_ref[b] >> 2]
    fetches[2].wait()
    fetches[3].wait()
    denom_ref[...] = denominator(
        blockmap_ref[b], groups, ab, c * share, share, ij, vir_ref[...], occ_ref
    )
    fetches[4].wait()
    value = ints_f32[...]
    high = value.astype(jnp.bfloat16)
    ints_hi[...] = high
    ints_lo[...] = (value - high.astype(jnp.float32)).astype(jnp.bfloat16)

    def sums_copy(j, to):
        return pltpu.make_async_remote_copy(
            src_ref=sums_out.at[j, to], dst_ref=sums_in.at[j, c],
            send_sem=s_send.at[j * nc + to], recv_sem=s_recv.at[j * nc + c],
            device_id=(b, to), device_id_type=MESH,
        )

    def sums_arrival(j, p):
        return pltpu.make_async_remote_copy(
            src_ref=sums_out.at[j, p], dst_ref=sums_in.at[j, p],
            send_sem=s_send.at[j * nc + p], recv_sem=s_recv.at[j * nc + p],
            device_id=(b, p), device_id_type=MESH,
        )

    lane = lax.broadcasted_iota(jnp.int32, (height, ij), 1)
    dot = functools.partial(lax.dot_general, dimension_numbers=NT, preferred_element_type=jnp.float32)
    sources = nb // CHUNKS

    def multiply(j):
        base = j * sources

        @pl.loop(base, base + sources)
        def _(p):
            @pl.when(p != b)
            def _():
                amps_arrival(p).wait_recv()

        for p in range(sources):
            for t in range(full):
                gathered[p * mine:(p + 1) * mine, t * LANES:(t + 1) * LANES] = (
                    inbox[base + p, t * mine:(t + 1) * mine, :]
                )
            row = inbox[base + p, full * mine:full * mine + 1, :]
            for u in range(mine):
                gathered[p * mine + u:p * mine + u + 1, full * LANES:cd] = row[:, u * rest:(u + 1) * rest]
        amps = gathered[...]
        amps_hi = amps.astype(jnp.bfloat16)
        amps_lo = (amps - amps_hi.astype(jnp.float32)).astype(jnp.bfloat16)
        both = jnp.concatenate([amps_hi] * CHUNKS + [amps_lo] * CHUNKS, axis=0)
        step = 160
        for r in range(0, ab, step):
            wide = dot(ints_hi[r:r + step, :], both)
            product[r:r + step, :] = (
                (dot(ints_lo[r:r + step, :], both[:ij]) + wide[:, ij:]) + wide[:, :ij]
            )
        for p in range(nc):
            rows = [product[p * share + start:p * share + start + height, :] for start in starts]
            block = rows[-1]
            for g in range(CHUNKS - 2, -1, -1):
                block = jnp.where(lane < (g + 1) * width, rows[g], block)
            sums_out[j, p] = block

        @pl.loop(1, nc)
        def _(k):
            sums_copy(j, (c + k) & (nc - 1)).start()

        sums_in[j, c] = sums_out[j, c]

    def add_up(j):
        @pl.loop(0, nc)
        def _(p):
            @pl.when(p != c)
            def _():
                sums_arrival(j, p).wait_recv()

        total = sums_in[j, 0]
        for p in range(1, nc):
            total = total + sums_in[j, p]
        totals[j] = total

    order = [0, 1, 3, 2] if CHUNKS == 4 else list(range(CHUNKS))
    for place, j in enumerate(order):
        multiply_at = j
        if place == 0:
            @pl.when(c < nc - 1)
            def _():
                pl.semaphore_wait(s_ready, nc - 1 - c)
        multiply(multiply_at)
    for j in order:
        add_up(j)

    for g, start in enumerate(starts):
        block = None
        for j in range(CHUNKS):
            turned = totals[j]
            if (j - g) % CHUNKS:
                turned = pltpu.roll(turned, (j - g) % CHUNKS * width, 1)
            block = turned if block is None else jnp.where(lane < j * width, block, turned)
        ladder_ref[start:start + height, 0, :] = block
        incr_ref[start:start + height, 0, :] = block / denom_ref[start:start + height, :]

    @pl.loop(0, nb)
    def _(p):
        @pl.when(p != b)
        def _():
            amps_copy(p).wait_send()

    for j in range(CHUNKS):
        @pl.loop(0, nc)
        def _(p):
            @pl.when(p != c)
            def _():
                sums_copy(j, p).wait_send()


def on_device(integrals, amplitudes, blockmap, vir_energy, occ_energy):
    nb, nc = lax.axis_size("blk"), lax.axis_size("ctr")
    _, ab, cd = integrals.shape
    irreps, _, mine = amplitudes.shape
    ij = mine * nb
    share = ab // nc
    height = -(-share // CHUNKS)
    rows = mine * cd // LANES
    vmem = pl.BlockSpec(memory_space=pltpu.VMEM)
    hbm = pl.BlockSpec(memory_space=pltpu.HBM)
    out = jax.ShapeDtypeStruct((share, 1, ij), jnp.float32)
    ladder, increment = pl.pallas_call(
        functools.partial(kernel, nb, nc),
        out_shape=(out, out),
        in_specs=[hbm] * 5,
        out_specs=(vmem, vmem),
        scratch_shapes=[
            pltpu.SMEM(blockmap.shape, jnp.int32),
            pltpu.SMEM(occ_energy.shape, jnp.float32),
            pltpu.VMEM((1, vir_energy.shape[0]), jnp.float32),
            pltpu.VMEM((irreps, mine, cd), jnp.float32),
            pltpu.VMEM((ab, cd), jnp.float32),
            pltpu.VMEM((ab, cd), jnp.bfloat16),
            pltpu.VMEM((ab, cd), jnp.bfloat16),
            pltpu.VMEM((irreps, rows, LANES), jnp.float32),
            pltpu.VMEM((nb, rows, LANES), jnp.float32),
            pltpu.VMEM((nb, rows, LANES), jnp.float32),
            pltpu.VMEM((ij // CHUNKS, cd), jnp.float32),
            pltpu.VMEM((ab, ij), jnp.float32),
            pltpu.VMEM((CHUNKS, nc, height, ij), jnp.float32),
            pltpu.VMEM((CHUNKS, nc, height, ij), jnp.float32),
            pltpu.VMEM((CHUNKS, height, ij), jnp.float32),
            pltpu.VMEM((share, ij), jnp.float32),
            pltpu.SemaphoreType.DMA((5,)),
            pltpu.SemaphoreType.DMA((nb,)),
            pltpu.SemaphoreType.DMA((nb,)),
            pltpu.SemaphoreType.DMA((CHUNKS * nc,)),
            pltpu.SemaphoreType.DMA((CHUNKS * nc,)),
            pltpu.SemaphoreType.REGULAR((nb,)),
            pltpu.SemaphoreType.REGULAR,
        ],
        compiler_params=pltpu.CompilerParams(
            collective_id=0, has_side_effects=True, vmem_limit_bytes=VLIM
        ),
    )(
        *(
            pltpu.with_memory_space_constraint(x, pltpu.HBM)
            for x in (blockmap, occ_energy, vir_energy, jnp.transpose(amplitudes, (0, 2, 1)), integrals[0])
        )
    )
    return jnp.transpose(ladder, (1, 0, 2)), jnp.transpose(increment, (1, 0, 2))


def solution(mesh):
    placed = (P("blk", None, "ctr"), P(None, "ctr", "blk"), P(), P(), P())
    return jax.shard_map(
        on_device,
        mesh=mesh,
        in_specs=placed,
        out_specs=(P("blk", "ctr", None), P("blk", "ctr", None)),
        check_vma=False,
    )
```

time: 51.5 us -> 46.3 us (0.90)
  the two profiles are of different devices: /device:TPU:352 before, /device:TPU:1 now
where the time goes in v3:
time: 46.3 us; the launch traced here: 46.1 us
  Pallas kernels  44.2 us (95%)
  local copies, waits for them, and re-layouts  1.22 us (3%)
  between operations  0.64 us (1%)
    pallas_call x1, Pallas kernels, on_device(): pl.pallas_call(functools.partial(kernel, nb, nc), out_shape=(out, out), i...  44.2 us
    unnamed x2, local copies, waits for them, and re-layouts  1.22 us

profile of v3, /device:TPU:1, one launch (start us, length us, event | category | flops | bytes accessed | tf_op | source)
XLA Modules:
  0.0 46.1 jit_solution(16538759288333698447)
XLA Ops:
  0.6 44.2 %shard_map.68 = (f32[50,1,128]{2,1,0:T(1,128)S(1)}, f32[50,1,128]{2,1,0:T(1,128)S(1)}) custom-call(s32[32]{0:T(128)} %blockmap_hbm.1, f32[32]{0:T(128)} %occ_hbm.1, f32[320]{0:T(512)} %vir_hbm.1, f32[8,4,800]{2,1,0:T(4,128)} %bitcast.7, f32[800,800]{1,0:T(8,128)} %bitcast.6), custom_call_target="tpu_custom_call" | custom-call | tf_op jit(solution)/shard_map/pallas_call | solution.py:293
  44.9 0.6 %copy.9 = f32[1,50,128]{2,0,1:T(1,128)} copy(f32[1,50,128]{2,0,1:T(1,128)S(1)} %bitcast.5) | data formatting | bytes 51200
  45.5 0.6 %copy.10 = f32[1,50,128]{2,0,1:T(1,128)} copy(f32[1,50,128]{2,0,1:T(1,128)S(1)} %bitcast.4) | data formatting | bytes 51200

commit v4 on v3

--- a/solution.py
+++ b/solution.py
@@ -63,6 +63,7 @@
     rank = rank_of(b)
     early = 14
     groups = nb // NIRR
+    sources = nb // CHUNKS
     ab, cd = ints_f32.shape
     share = ab // nc
     irreps, mine, _ = amps_ref.shape
@@ -115,14 +116,8 @@
 
     def amps_copy(to):
         return pltpu.make_async_remote_copy(
-            src_ref=outbox.at[to], dst_ref=inbox.at[b], send_sem=a_send.at[to], recv_sem=a_recv.at[b],
+            src_ref=outbox.at[to], dst_ref=inbox.at[b], send_sem=a_send, recv_sem=a_recv.at[b // sources],
             device_id=(to, c), device_id_type=MESH,
-        )
-
-    def amps_arrival(p):
-        return pltpu.make_async_remote_copy(
-            src_ref=outbox.at[p], dst_ref=inbox.at[p], send_sem=a_send.at[p], recv_sem=a_recv.at[p],
-            device_id=(p, c), device_id_type=MESH,
         )
 
     def visit(to):
@@ -162,7 +157,8 @@
         def _():
             visit(to)
 
-    inbox[b] = packed[blockmap_ref[b] >> 2]
+    outbox[b] = packed[blockmap_ref[b] >> 2]
+    pltpu.make_async_copy(outbox.at[b], inbox.at[b], a_recv.at[b // sources]).start()
     fetches[2].wait()
     fetches[3].wait()
     denom_ref[...] = denominator(
@@ -177,29 +173,18 @@
     def sums_copy(j, to):
         return pltpu.make_async_remote_copy(
             src_ref=sums_out.at[j, to], dst_ref=sums_in.at[j, c],
-            send_sem=s_send.at[j * nc + to], recv_sem=s_recv.at[j * nc + c],
+            send_sem=s_send.at[j], recv_sem=s_recv.at[j],
             device_id=(b, to), device_id_type=MESH,
-        )
-
-    def sums_arrival(j, p):
-        return pltpu.make_async_remote_copy(
-            src_ref=sums_out.at[j, p], dst_ref=sums_in.at[j, p],
-            send_sem=s_send.at[j * nc + p], recv_sem=s_recv.at[j * nc + p],
-            device_id=(b, p), device_id_type=MESH,
         )
 
     lane = lax.broadcasted_iota(jnp.int32, (height, ij), 1)
     dot = functools.partial(lax.dot_general, dimension_numbers=NT, preferred_element_type=jnp.float32)
-    sources = nb // CHUNKS
 
     def multiply(j):
         base = j * sources
 
-        @pl.loop(base, base + sources)
-        def _(p):
-            @pl.when(p != b)
-            def _():
-                amps_arrival(p).wait_recv()
+        arrived = inbox.at[pl.ds(base, sources)]
+        pltpu.make_async_copy(arrived, arrived, a_recv.at[j]).wait()
 
         for p in range(sources):
             for t in range(full):
@@ -230,15 +215,10 @@
         def _(k):
             sums_copy(j, (c + k) & (nc - 1)).start()
 
-        sums_in[j, c] = sums_out[j, c]
+        pltpu.make_async_copy(sums_out.at[j, c], sums_in.at[j, c], s_recv.at[j]).start()
 
     def add_up(j):
-        @pl.loop(0, nc)
-        def _(p):
-            @pl.when(p != c)
-            def _():
-                sums_arrival(j, p).wait_recv()
-
+        pltpu.make_async_copy(sums_in.at[j], sums_in.at[j], s_recv.at[j]).wait()
         total = sums_in[j, 0]
         for p in range(1, nc):
             total = total + sums_in[j, p]
@@ -252,6 +232,11 @@
             def _():
                 pl.semaphore_wait(s_ready, nc - 1 - c)
         multiply(multiply_at)
+    sent = outbox.at[pl.ds(0, nb - 1)]
+    pltpu.make_async_copy(sent, sent, a_send).wait()
+    for j in order:
+        sent = sums_out.at[j, pl.ds(0, nc - 1)]
+        pltpu.make_async_copy(sent, sent, s_send.at[j]).wait()
     for j in order:
         add_up(j)
 
@@ -264,19 +249,6 @@
             block = turned if block is None else jnp.where(lane < j * width, block, turned)
         ladder_ref[start:start + height, 0, :] = block
         incr_ref[start:start + height, 0, :] = block / denom_ref[start:start + height, :]
-
-    @pl.loop(0, nb)
-    def _(p):
-        @pl.when(p != b)
-        def _():
-            amps_copy(p).wait_send()
-
-    for j in range(CHUNKS):
-        @pl.loop(0, nc)
-        def _(p):
-            @pl.when(p != c)
-            def _():
-                sums_copy(j, p).wait_send()
 
 
 def on_device(integrals, amplitudes, blockmap, vir_energy, occ_energy):
@@ -313,10 +285,10 @@
             pltpu.VMEM((CHUNKS, height, ij), jnp.float32),
             pltpu.VMEM((share, ij), jnp.float32),
             pltpu.SemaphoreType.DMA((5,)),
-            pltpu.SemaphoreType.DMA((nb,)),
-            pltpu.SemaphoreType.DMA((nb,)),
-            pltpu.SemaphoreType.DMA((CHUNKS * nc,)),
-            pltpu.SemaphoreType.DMA((CHUNKS * nc,)),
+            pltpu.SemaphoreType.DMA,
+            pltpu.SemaphoreType.DMA((CHUNKS,)),
+            pltpu.SemaphoreType.DMA((CHUNKS,)),
+            pltpu.SemaphoreType.DMA((CHUNKS,)),
             pltpu.SemaphoreType.REGULAR((nb,)),
             pltpu.SemaphoreType.REGULAR,
         ],

time: 46.3 us -> 44.8 us (0.968)
  Pallas kernels: 44.2 us -> 42.7 us
    pallas_call x1, Pallas kernels: 44.2 us -> 42.7 us  [on_device(): pl.pallas_call(functools.partial(kernel, nb, nc), out_shape=(out, out), i...]
where the time goes in v4:
time: 44.8 us; the launch traced here: 44.6 us
  Pallas kernels  42.7 us (95%)
  local copies, waits for them, and re-layouts  1.22 us (3%)
  between operations  0.64 us (1%)
    pallas_call x1, Pallas kernels, on_device(): pl.pallas_call(functools.partial(kernel, nb, nc), out_shape=(out, out), i...  42.7 us
    unnamed x2, local copies, waits for them, and re-layouts  1.22 us

profile of v4, /device:TPU:1, one launch (start us, length us, event | category | flops | bytes accessed | tf_op | source)
XLA Modules:
  0.0 44.6 jit_solution(18098525797968934776)
XLA Ops:
  0.6 42.7 %shard_map.68 = (f32[50,1,128]{2,1,0:T(1,128)S(1)}, f32[50,1,128]{2,1,0:T(1,128)S(1)}) custom-call(s32[32]{0:T(128)} %blockmap_hbm.1, f32[32]{0:T(128)} %occ_hbm.1, f32[320]{0:T(512)} %vir_hbm.1, f32[8,4,800]{2,1,0:T(4,128)} %bitcast.7, f32[800,800]{1,0:T(8,128)} %bitcast.6), custom_call_target="tpu_custom_call" | custom-call | tf_op jit(solution)/shard_map/pallas_call | solution.py:265
  43.4 0.6 %copy.9 = f32[1,50,128]{2,0,1:T(1,128)} copy(f32[1,50,128]{2,0,1:T(1,128)S(1)} %bitcast.5) | data formatting | bytes 51200
  44.0 0.6 %copy.10 = f32[1,50,128]{2,0,1:T(1,128)} copy(f32[1,50,128]{2,0,1:T(1,128)S(1)} %bitcast.4) | data formatting | bytes 51200

commit v5 on v4

--- a/solution.py
+++ b/solution.py
@@ -97,9 +97,10 @@
     def _():
         pl.semaphore_wait(barrier, rank + c)
 
-    @pl.loop(0, rank)
-    def _(r):
-        pl.semaphore_signal(a_ready.at[b], inc=1, device_id=(at_rank(r), c), device_id_type=MESH)
+    for p in range(nb):
+        @pl.when(rank_of(jnp.int32(p)) < rank)
+        def _():
+            pl.semaphore_signal(a_ready.at[b], inc=1, device_id=(p, c), device_id_type=MESH)
 
     @pl.loop(0, c)
     def _(p):
@@ -199,21 +200,31 @@
         amps_lo = (amps - amps_hi.astype(jnp.float32)).astype(jnp.bfloat16)
         both = jnp.concatenate([amps_hi] * CHUNKS + [amps_lo] * CHUNKS, axis=0)
         step = 160
-        for r in range(0, ab, step):
+
+        def rows_of(r):
             wide = dot(ints_hi[r:r + step, :], both)
             product[r:r + step, :] = (
                 (dot(ints_lo[r:r + step, :], both[:ij]) + wide[:, ij:]) + wide[:, :ij]
             )
-        for p in range(nc):
+
+        def pack(p):
             rows = [product[p * share + start:p * share + start + height, :] for start in starts]
             block = rows[-1]
             for g in range(CHUNKS - 2, -1, -1):
                 block = jnp.where(lane < (g + 1) * width, rows[g], block)
             sums_out[j, p] = block
 
-        @pl.loop(1, nc)
-        def _(k):
-            sums_copy(j, (c + k) & (nc - 1)).start()
+        done = 0
+        for r in range(0, ab, step):
+            rows_of(r)
+            ready = (r + step) // share
+            for p in range(done, ready):
+                pack(p)
+            for p in range(done, ready):
+                @pl.when(p != c)
+                def _():
+                    sums_copy(j, p).start()
+            done = ready
 
         pltpu.make_async_copy(sums_out.at[j, c], sums_in.at[j, c], s_recv.at[j]).start()
 

time: 44.8 us -> 43.5 us (0.971)
  Pallas kernels: 42.7 us -> 41.2 us
    pallas_call x1, Pallas kernels: 42.7 us -> 41.2 us  [on_device(): pl.pallas_call(functools.partial(kernel, nb, nc), out_shape=(out, out), i...]
where the time goes in v5:
time: 43.5 us; the launch traced here: 43 us
  Pallas kernels  41.2 us (95%)
  local copies, waits for them, and re-layouts  1.22 us (3%)
  between operations  0.64 us (1%)
    pallas_call x1, Pallas kernels, on_device(): pl.pallas_call(functools.partial(kernel, nb, nc), out_shape=(out, out), i...  41.2 us
    unnamed x2, local copies, waits for them, and re-layouts  1.22 us

profile of v5, /device:TPU:1, one launch (start us, length us, event | category | flops | bytes accessed | tf_op | source)
XLA Modules:
  0.0 43.0 jit_solution(13521117104793134613)
XLA Ops:
  0.6 41.2 %shard_map.68 = (f32[50,1,128]{2,1,0:T(1,128)S(1)}, f32[50,1,128]{2,1,0:T(1,128)S(1)}) custom-call(s32[32]{0:T(128)} %blockmap_hbm.1, f32[32]{0:T(128)} %occ_hbm.1, f32[320]{0:T(512)} %vir_hbm.1, f32[8,4,800]{2,1,0:T(4,128)} %bitcast.7, f32[800,800]{1,0:T(8,128)} %bitcast.6), custom_call_target="tpu_custom_call" | custom-call | tf_op jit(solution)/shard_map/pallas_call | solution.py:276
  41.8 0.6 %copy.9 = f32[1,50,128]{2,0,1:T(1,128)} copy(f32[1,50,128]{2,0,1:T(1,128)S(1)} %bitcast.5) | data formatting | bytes 51200
  42.4 0.6 %copy.10 = f32[1,50,128]{2,0,1:T(1,128)} copy(f32[1,50,128]{2,0,1:T(1,128)S(1)} %bitcast.4) | data formatting | bytes 51200

commit v6 on v5

--- a/solution.py
+++ b/solution.py
@@ -53,10 +53,10 @@
 
 def kernel(
     nb, nc, blockmap_hbm, occ_hbm, vir_hbm, amps_hbm, ints_hbm,
-    ladder_ref, incr_ref,
+    half_one_ref, half_two_ref, denom_ref,
     blockmap_ref, occ_ref, vir_ref, amps_ref,
     ints_f32, ints_hi, ints_lo, packed, outbox, inbox, gathered, product, sums_out, sums_in,
-    totals, denom_ref, fetch_sem, a_send, a_recv, s_send, s_recv, a_ready, s_ready,
+    totals, fetch_sem, a_send, a_recv, s_send, s_recv, a_ready, s_ready,
 ):
     b = lax.axis_index("blk")
     c = lax.axis_index("ctr")
@@ -162,7 +162,7 @@
     pltpu.make_async_copy(outbox.at[b], inbox.at[b], a_recv.at[b // sources]).start()
     fetches[2].wait()
     fetches[3].wait()
-    denom_ref[...] = denominator(
+    denom_ref[:, 0, :] = denominator(
         blockmap_ref[b], groups, ab, c * share, share, ij, vir_ref[...], occ_ref
     )
     fetches[4].wait()
@@ -230,10 +230,11 @@
 
     def add_up(j):
         pltpu.make_async_copy(sums_in.at[j], sums_in.at[j], s_recv.at[j]).wait()
-        total = sums_in[j, 0]
-        for p in range(1, nc):
-            total = total + sums_in[j, p]
-        totals[j] = total
+        for half in range(2):
+            total = sums_in[j, half * nc // 2]
+            for p in range(half * nc // 2 + 1, (half + 1) * nc // 2):
+                total = total + sums_in[j, p]
+            totals[half, j] = total
 
     order = [0, 1, 3, 2] if CHUNKS == 4 else list(range(CHUNKS))
     for place, j in enumerate(order):
@@ -251,15 +252,15 @@
     for j in order:
         add_up(j)
 
-    for g, start in enumerate(starts):
-        block = None
-        for j in range(CHUNKS):
-            turned = totals[j]
-            if (j - g) % CHUNKS:
-                turned = pltpu.roll(turned, (j - g) % CHUNKS * width, 1)
-            block = turned if block is None else jnp.where(lane < j * width, block, turned)
-        ladder_ref[start:start + height, 0, :] = block
-        incr_ref[start:start + height, 0, :] = block / denom_ref[start:start + height, :]
+    for half, half_ref in enumerate([half_one_ref, half_two_ref]):
+        for g, start in enumerate(starts):
+            block = None
+            for j in range(CHUNKS):
+                turned = totals[half, j]
+                if (j - g) % CHUNKS:
+                    turned = pltpu.roll(turned, (j - g) % CHUNKS * width, 1)
+                block = turned if block is None else jnp.where(lane < j * width, block, turned)
+            half_ref[start:start + height, 0, :] = block
 
 
 def on_device(integrals, amplitudes, blockmap, vir_energy, occ_energy):
@@ -273,11 +274,11 @@
     vmem = pl.BlockSpec(memory_space=pltpu.VMEM)
     hbm = pl.BlockSpec(memory_space=pltpu.HBM)
     out = jax.ShapeDtypeStruct((share, 1, ij), jnp.float32)
-    ladder, increment = pl.pallas_call(
+    half_one, half_two, denom = pl.pallas_call(
         functools.partial(kernel, nb, nc),
-        out_shape=(out, out),
+        out_shape=(out, out, out),
         in_specs=[hbm] * 5,
-        out_specs=(vmem, vmem),
+        out_specs=(vmem, vmem, vmem),
         scratch_shapes=[
             pltpu.SMEM(blockmap.shape, jnp.int32),
             pltpu.SMEM(occ_energy.shape, jnp.float32),
@@ -293,8 +294,7 @@
             pltpu.VMEM((ab, ij), jnp.float32),
             pltpu.VMEM((CHUNKS, nc, height, ij), jnp.float32),
             pltpu.VMEM((CHUNKS, nc, height, ij), jnp.float32),
-            pltpu.VMEM((CHUNKS, height, ij), jnp.float32),
-            pltpu.VMEM((share, ij), jnp.float32),
+            pltpu.VMEM((2, CHUNKS, height, ij), jnp.float32),
             pltpu.SemaphoreType.DMA((5,)),
             pltpu.SemaphoreType.DMA,
             pltpu.SemaphoreType.DMA((CHUNKS,)),
@@ -312,7 +312,8 @@
             for x in (blockmap, occ_energy, vir_energy, jnp.transpose(amplitudes, (0, 2, 1)), integrals[0])
         )
     )
-    return jnp.transpose(ladder, (1, 0, 2)), jnp.transpose(increment, (1, 0, 2))
+    ladder = half_one + half_two
+    return jnp.transpose(ladder, (1, 0, 2)), jnp.transpose(ladder / denom, (1, 0, 2))
 
 
 def solution(mesh):

time: 43.5 us -> 42.9 us (0.986)
  local copies, waits for them, and re-layouts: 1.22 us -> 0 us
  other arithmetic: 0 us -> 0.66 us
    unnamed x2 -> x0, local copies, waits for them, and re-layouts: 1.22 us -> none
    transpose x0 -> x1, other arithmetic: none -> 0.66 us  [on_device(): jnp.transpose(ladder / denom, (1, 0, 2))]
where the time goes in v6:
time: 42.9 us; the launch traced here: 42.4 us
  Pallas kernels  41.1 us (96%)
  other arithmetic  0.66 us (2%)
  between operations  0.64 us (1%)
    pallas_call x1, Pallas kernels, on_device(): pl.pallas_call(functools.partial(kernel, nb, nc), out_shape=(out, out, ou...  41.1 us

profile of v6, /device:TPU:1, one launch (start us, length us, event | category | flops | bytes accessed | tf_op | source)
XLA Modules:
  0.0 42.4 jit_solution(12632449158232484119)
XLA Ops:
  0.6 41.1 %shard_map.68 = (f32[50,1,128]{2,1,0:T(1,128)S(1)}, f32[50,1,128]{2,1,0:T(1,128)S(1)}, f32[50,1,128]{2,1,0:T(1,128)S(1)}) custom-call(s32[32]{0:T(128)} %blockmap_hbm.1, f32[32]{0:T(128)} %occ_hbm.1, f32[320]{0:T(512)} %vir_hbm.1, f32[8,4,800]{2,1,0:T(4,128)} %bitcast.7, f32[800,800]{1,0:T(8,128)} %bitcast.6), custom_call_target="tpu_custom_call" | custom-call | tf_op jit(solution)/shard_map/pallas_call | solution.py:277
  41.8 0.7 %divide_bitcast_fusion = (f32[1,50,128]{2,0,1:T(1,128)}, f32[1,50,128]{2,0,1:T(1,128)}) fusion(f32[50,1,128]{2,1,0:T(1,128)S(1)} %get-tuple-element.7, f32[50,1,128]{2,1,0:T(1,128)S(1)} %get-tuple-element.5, f32[50,1,128]{2,1,0:T(1,128)S(1)} %get-tuple-element.6), kind=kLoop, calls=%fused_computation | loop fusion | flops 12800 | bytes 128000 | tf_op jit(solution)/shard_map/transpose | solution.py:316

commit v7 on v6

--- a/solution.py
+++ b/solution.py
@@ -61,7 +61,7 @@
     b = lax.axis_index("blk")
     c = lax.axis_index("ctr")
     rank = rank_of(b)
-    early = 14
+    early = 15
     groups = nb // NIRR
     sources = nb // CHUNKS
     ab, cd = ints_f32.shape
@@ -244,13 +244,14 @@
             def _():
                 pl.semaphore_wait(s_ready, nc - 1 - c)
         multiply(multiply_at)
+    for j in order[:-1]:
+        add_up(j)
     sent = outbox.at[pl.ds(0, nb - 1)]
     pltpu.make_async_copy(sent, sent, a_send).wait()
     for j in order:
         sent = sums_out.at[j, pl.ds(0, nc - 1)]
         pltpu.make_async_copy(sent, sent, s_send.at[j]).wait()
-    for j in order:
-        add_up(j)
+    add_up(order[-1])
 
     for half, half_ref in enumerate([half_one_ref, half_two_ref]):
         for g, start in enumerate(starts):

time: 42.9 us -> 42.8 us (level)
  no operation moved by 1% of the time
where the time goes in v7:
time: 42.8 us; the launch traced here: 42.5 us
  Pallas kernels  41.2 us (96%)
  other arithmetic  0.66 us (2%)
  between operations  0.64 us (1%)
    pallas_call x1, Pallas kernels, on_device(): pl.pallas_call(functools.partial(kernel, nb, nc), out_shape=(out, out, ou...  41.2 us

profile of v7, /device:TPU:1, one launch (start us, length us, event | category | flops | bytes accessed | tf_op | source)
XLA Modules:
  0.0 42.5 jit_solution(9156810891628017579)
XLA Ops:
  0.6 41.2 %shard_map.68 = (f32[50,1,128]{2,1,0:T(1,128)S(1)}, f32[50,1,128]{2,1,0:T(1,128)S(1)}, f32[50,1,128]{2,1,0:T(1,128)S(1)}) custom-call(s32[32]{0:T(128)} %blockmap_hbm.1, f32[32]{0:T(128)} %occ_hbm.1, f32[320]{0:T(512)} %vir_hbm.1, f32[8,4,800]{2,1,0:T(4,128)} %bitcast.7, f32[800,800]{1,0:T(8,128)} %bitcast.6), custom_call_target="tpu_custom_call" | custom-call | tf_op jit(solution)/shard_map/pallas_call | solution.py:278
  41.8 0.7 %divide_bitcast_fusion = (f32[1,50,128]{2,0,1:T(1,128)}, f32[1,50,128]{2,0,1:T(1,128)}) fusion(f32[50,1,128]{2,1,0:T(1,128)S(1)} %get-tuple-element.7, f32[50,1,128]{2,1,0:T(1,128)S(1)} %get-tuple-element.5, f32[50,1,128]{2,1,0:T(1,128)S(1)} %get-tuple-element.6), kind=kLoop, calls=%fused_computation | loop fusion | flops 12800 | bytes 128000 | tf_op jit(solution)/shard_map/transpose | solution.py:317
